TPU v7x, 32 devices: a whole 2x2x4 slice. The times are simulated.
32 devices in a mesh: gy: 4 (over x, core), gz: 2 (over y), ga: 4 (over z).
Axes of the slice: x: 2, y: 2, z: 4, core: 2. Of those that a mesh axis runs over, the one named last changes fastest.
Arguments:
- fields: float32 [16, 256, 8, 512], P(None, 'gy', 'gz', 'ga'), may hold values from -6 to 6
- section_start: float32 [16, 256, 8, 512], P(None, 'gy', 'gz', 'ga'), may hold values from -6 to 6
- velocity: float32 [3, 256, 8, 512], P(None, 'gy', 'gz', 'ga'), may hold values from -4 to 4
- diffusivity: float32 [16], replicated, may hold values from 0.02 to 0.2
- reaction: float32 [16, 16], replicated, may hold values from -1.5 to 1.5
- x_factor: bfloat16 [512, 64], replicated, may hold values from -0.25 to 0.25
- y_factor: float32 [256, 64], replicated, may hold values from -6 to 6
Outputs:
- new_fields: float32 [16, 256, 8, 512], P(None, 'gy', 'gz', 'ga')
- x_gram: float32 [512, 512], P(('gy', 'gz'))
- y_products: float32 [8, 256, 64], P(('gz', 'gy'))
All inputs are finite; a program needn't handle non-finite values.
Results may differ from a plain program's by a relative error of at most 0.0028.
Values may be sent and summed in bfloat16 or wider, within the bound.
No kernel may reach another device: no remote copies, remote signals or barrier semaphores. Data moves between devices by JAX's collectives and lax.ppermute only.
A program may use at most 64 MiB of HBM per device.

v0:
```python
import jax
import jax.numpy as jnp
from jax import lax
from jax.sharding import PartitionSpec as P

time_step = 0.4


def with_halo(block, sides, width):
    for axis, dim in sides:
        count = lax.axis_size(axis)
        forward = [(i, i + 1) for i in range(count - 1)]
        backward = [(target, source) for source, target in forward]
        low = lax.ppermute(
            lax.slice_in_dim(block, block.shape[dim] - width, None, axis=dim), axis, forward
        )
        high = lax.ppermute(lax.slice_in_dim(block, 0, width, axis=dim), axis, backward)
        block = jnp.concatenate([low, block, high], axis=dim)
    return block


def shards(fields, section_start, velocity, diffusivity, reaction, x_factor, y_factor):
    padded = with_halo(fields, (("gy", 1), ("gz", 2), ("ga", 3)), 1)
    center = padded[:, 1:-1, 1:-1, 1:-1]
    y_plus = padded[:, 2:, 1:-1, 1:-1]
    y_minus = padded[:, :-2, 1:-1, 1:-1]
    z_plus = padded[:, 1:-1, 2:, 1:-1]
    z_minus = padded[:, 1:-1, :-2, 1:-1]
    x_plus = padded[:, 1:-1, 1:-1, 2:]
    x_minus = padded[:, 1:-1, 1:-1, :-2]
    laplace_sum = y_plus + y_minus + z_plus + z_minus + x_plus + x_minus - 6.0 * center
    advection = (
        velocity[0][None] * (x_plus - x_minus) * 0.5
        + velocity[1][None] * (y_plus - y_minus) * 0.5
        + velocity[2][None] * (z_plus - z_minus) * 0.5
    )
    diffusion = diffusivity[:, None, None, None]
    tendency = (
        diffusion * laplace_sum
        - advection
        + jnp.einsum("vw,wyzx->vyzx", reaction, fields, precision=lax.Precision.HIGHEST)
    )
    section_value = 0.75 * section_start + 0.25 * (fields + time_step * tendency)
    buffer_rank = lax.axis_index("ga") == lax.axis_size("ga") - 1
    new_fields = jnp.where(buffer_rank, fields, section_value)
    snapshot = new_fields.astype(jnp.bfloat16)
    devices = lax.axis_size("gy") * lax.axis_size("gz")
    rank_x = x_factor.shape[1]
    gathered = lax.all_gather(snapshot, "ga", axis=3, tiled=True)
    variables, y_cells, z_cells, x_cells = gathered.shape
    unfolded = gathered.reshape(variables * y_cells * z_cells, x_cells)
    cell_count = float(variables * y_cells * z_cells * devices)
    gram_rows = lax.psum_scatter(
        lax.dot_general(
            unfolded, unfolded, (((0,), (0,)), ((), ())), preferred_element_type=jnp.float32
        ),
        ("gy", "gz"),
        scatter_dimension=0,
        tiled=True,
    )
    x_gram = gram_rows / cell_count
    projected = jnp.einsum(
        "vyzx,xr->yzvr", gathered, x_factor, preferred_element_type=jnp.float32
    ).astype(jnp.bfloat16)
    projected = projected.reshape(y_cells, z_cells, variables * rank_x)
    full_y = lax.all_to_all(projected, "gy", split_axis=1, concat_axis=0, tiled=True)
    y_gram = jnp.einsum("yzc,wzc->zyw", full_y, full_y, preferred_element_type=jnp.float32) / float(
        variables * rank_x
    )
    y_products = jnp.einsum("zyw,wk->zyk", y_gram, y_factor, precision=lax.Precision.HIGHEST)
    return (new_fields, x_gram, y_products)


def solution(mesh):
    in_specs = (
        P(None, "gy", "gz", "ga"),
        P(None, "gy", "gz", "ga"),
        P(None, "gy", "gz", "ga"),
        P(),
        P(),
        P(),
        P(),
    )
    out_specs = (P(None, "gy", "gz", "ga"), P(("gy", "gz"), None), P(("gz", "gy"), None, None))
    return jax.shard_map(shards, mesh=mesh, in_specs=in_specs, out_specs=out_specs, check_vma=False)
```

profile of v0, /device:TPU:0, one launch (start us, length us, event | category | flops | bytes accessed | tf_op | source)
XLA Modules:
  0.0 199.7 jit_solution(294682262062690017)
XLA Ops:
  7.2 3.0 %copy.52 = f32[16,64,4,128]{3,0,2,1:T(8,128)S(1)} copy(f32[16,64,4,128]{3,2,1,0:T(4,128)} %param.7) | data formatting | bytes 4194304 | tf_op args[0]
  10.2 2.4 %collective-permute-start.1 = (f32[16,1,4,128]{3,0,2,1:T(8,128)S(1)}, f32[16,1,4,128]{3,0,2,1:T(8,128)S(1)}, u32[]{:S(2)}, u32[]{:S(2)}) collective-permute-start(f32[16,1,4,128]{3,0,2,1:T(8,128)S(1)} %get-tuple-element.17), channel_id=1, source_target_pairs={{0,8},{8,16},{16,24},{1,9},{9,17},{17,25},{2,10},{10,18},{18,26},{... | collective-permute-start | bytes 98312 | tf_op jit(solution)/shard_map/ppermute | solution.py:14
  15.2 2.6 %collective-permute-done = f32[16,1,4,128]{3,0,2,1:T(8,128)S(1)} collective-permute-done((f32[16,1,4,128]{3,0,2,1:T(8,128)S(1)}, f32[16,1,4,128]{3,0,2,1:T(8,128)S(1)}, u32[]{:S(2)}, u32[]{:S(2)}) %collective-permute-start) | collective-permute-done | bytes 32800 | tf_op jit(solution)/shard_map/ppermute | solution.py:17
  17.9 1.3 collective-permute-start.2
  19.2 4.6 %collective-permute-start.3 = (f32[16,66,1,128]{3,0,2,1:T(8,128)S(1)}, f32[16,66,1,128]{3,0,2,1:T(8,128)S(1)}, u32[]{:S(2)}, u32[]{:S(2)}) collective-permute-start(f32[16,66,1,128]{3,0,2,1:T(8,128)S(1)} %get-tuple-element.14), channel_id=1, source_target_pairs={{0,4},{1,5},{2,6},{3,7},{8,12},{9,13},{10,14},{11,15},{16,20},{17,... | collective-permute-start | bytes 1622024 | tf_op jit(solution)/shard_map/ppermute | solution.py:14
  23.8 9.5 %collective-permute-done.2 = f32[16,66,1,128]{3,0,2,1:T(8,128)S(1)} collective-permute-done((f32[16,66,1,128]{3,0,2,1:T(8,128)S(1)}, f32[16,66,1,128]{3,0,2,1:T(8,128)S(1)}, u32[]{:S(2)}, u32[]{:S(2)}) %collective-permute-start.2) | collective-permute-done | bytes 540704 | tf_op jit(solution)/shard_map/ppermute | solution.py:17
  33.3 1.8 collective-permute-done.3
  36.2 2.9 %fusion.12 = (f32[16,66,6,1]{3,0,2,1:T(8,128)}, f32[16,66,6,1]{3,0,2,1:T(8,128)S(1)}) fusion(f32[16,66,6,128]{3,0,2,1:T(8,128)S(1)} %pad_maximum_fusion), kind=kLoop, calls=%fused_computation.30 | loop fusion | bytes 101376 | tf_op jit(solution)/shard_map/slice | solution.py:17
  39.0 2.8 %copy.45 = f32[16,66,6,1]{1,0,3,2:T(8,128)S(1)} copy(f32[16,66,6,1]{3,0,2,1:T(8,128)} %get-tuple-element.12) | data formatting | bytes 50688 | tf_op jit(solution)/shard_map/slice | solution.py:17
  43.1 2.2 %copy.47 = f32[16,66,6,1]{1,0,3,2:T(8,128)} copy(f32[16,66,6,1]{3,0,2,1:T(8,128)S(1)} %get-tuple-element.13) | data formatting | bytes 50688 | tf_op jit(solution)/shard_map/slice | solution.py:15
  45.3 5.2 %collective-permute-start.5 = (f32[16,66,6,1]{1,0,3,2:T(8,128)}, f32[16,66,6,1]{1,0,3,2:T(8,128)}, u32[]{:S(2)}, u32[]{:S(2)}) collective-permute-start(f32[16,66,6,1]{1,0,3,2:T(8,128)} %copy.47), channel_id=1, source_target_pairs={{0,1},{1,2},{2,3},{4,5},{5,6},{6,7},{8,9},{9,10},{10,11},{12,13},{... | collective-permute-start | bytes 76040 | tf_op jit(solution)/shard_map/ppermute | solution.py:14
  50.5 1.8 slice_bitcast_fusion.2
  52.2 2.6 %copy.46 = f32[16,66,6,1]{3,0,2,1:T(8,128)} copy(f32[16,66,6,1]{1,0,3,2:T(8,128)S(1)} %collective-permute-done.4) | data formatting | bytes 50688 | tf_op jit(solution)/shard_map/ppermute | solution.py:17
  54.9 3.6 %copy.48 = f32[16,66,6,1]{3,0,2,1:T(8,128)} copy(f32[16,66,6,1]{1,0,3,2:T(8,128)} %collective-permute-done.5) | data formatting | bytes 50688 | tf_op jit(solution)/shard_map/ppermute | solution.py:14
  58.5 10.6 %fusion.15 = (bf16[16,64,4,128]{3,0,2,1:T(8,128)(2,1)}, f32[16,64,4,128]{3,0,2,1:T(8,128)}) fusion(f32[16,64,4,128]{3,0,2,1:T(8,128)} %copy-done.4, f32[16,16]{1,0:T(8,128)S(1)} %copy-done.14, f32[64,4,128]{2,1,0:T(4,128)} %get-tuple-element.19, f32[64,4,128]{2,1,0:T(4,128)} %get-tuple-element.20, f32[64,4,128]{2,1,0:T(4,128)S(1)} %get-tuple-element.18, ...), kind=kOutput, calls=%fused_computation.33 | convolution fusion | flops 119537664 | bytes 11094593 | tf_op jit(solution)/shard_map/vw,wyzx->vyzx/dot_general | solution.py:41
  69.4 80.7 %all-gather.2.cloned.1.call-done = bf16[16,64,4,512]{3,0,2,1:T(8,128)(2,1)} async-done(((bf16[16,64,4,128]{3,0,2,1:T(8,128)(2,1)}), bf16[16,64,4,512]{3,0,2,1:T(8,128)(2,1)}) %all-gather.2.cloned.1.call-update) | async-done | bytes 4194320 | tf_op jit(solution)/shard_map/all_gather | solution.py:49
  150.1 6.8 %convolution_bitcast_fusion = f32[512,512]{1,0:T(8,128)} fusion(bf16[16,64,4,512]{3,0,2,1:T(8,128)(2,1)} %all-gather.2.cloned.1.call-done), kind=kOutput, calls=%fused_computation.18 | convolution fusion | flops 2147483648 | bytes 5242880 | tf_op jit(solution)/shard_map/dot_general | solution.py:54
  157.0 6.9 %fusion.7 = bf16[64,4,16,64]{3,0,1,2:T(8,128)(2,1)S(1)} fusion(bf16[16,64,4,512]{3,0,2,1:T(8,128)(2,1)} %all-gather.2.cloned.1.call-done, bf16[512,64]{0,1:T(8,128)(2,1)S(1)} %copy-done), kind=kOutput, calls=%fused_computation.17 | convolution fusion | flops 268697600 | bytes 4784128 | tf_op jit(solution)/shard_map/vyzx,xr->yzvr/dot_general | solution.py:62
  164.6 1.5 reshape.22
  166.1 3.5 %all-to-all-start = ((bf16[64,4,1024]{2,0,1:T(8,128)(2,1)}), bf16[64,4,1024]{2,0,1:T(8,128)(2,1)S(1)}, u32[]{:S(2)}, u32[]{:S(2)}) async-start(bf16[64,4,1024]{2,0,1:T(8,128)(2,1)} %reshape.22), calls=%async_computation.1 | async-start | bytes 1048576 | tf_op jit(solution)/shard_map/all_to_all | solution.py:66
  169.6 2.1 %copy.55 = f32[16,64,4,128]{3,2,1,0:T(4,128)} copy(f32[16,64,4,128]{3,0,2,1:T(8,128)S(1)} %copy-done.5) | data formatting | bytes 4194304
  171.7 8.1 %all-to-all-done = bf16[64,4,1024]{2,0,1:T(8,128)(2,1)S(1)} async-done(((bf16[64,4,1024]{2,0,1:T(8,128)(2,1)}), bf16[64,4,1024]{2,0,1:T(8,128)(2,1)S(1)}, u32[]{:S(2)}, u32[]{:S(2)}) %all-to-all-start) | async-done | bytes 524320 | tf_op jit(solution)/shard_map/all_to_all | solution.py:66
  181.2 10.1 %reduce-scatter.2.cloned.1.call-done = f32[64,512]{1,0:T(8,128)} async-done(((f32[512,512]{1,0:T(8,128)}), f32[64,512]{1,0:T(8,128)}) %reduce-scatter.2.cloned.1.call-update) | async-done | bytes 131088 | tf_op jit(solution)/shard_map/reduce_scatter | solution.py:53
  191.3 1.6 broadcast_multiply_fusion
  (50 shorter events, 7.4 us)
Async XLA Ops:
  7.2 149.8 %copy-start = (bf16[512,64]{0,1:T(8,128)(2,1)S(1)}, bf16[512,64]{0,1:T(8,128)(2,1)}, u32[]{:S(2)}) copy-start(bf16[512,64]{0,1:T(8,128)(2,1)} %param.12) | copy-start | bytes 196612
  7.2 6.8 %copy-start.1 = (f32[16,64,4,128]{3,2,1,0:T(4,128)S(1)}, f32[16,64,4,128]{3,2,1,0:T(4,128)}, u32[]{:S(2)}) copy-start(f32[16,64,4,128]{3,2,1,0:T(4,128)} %param.7) | copy-start | bytes 6291460
  7.2 142.9 %all-gather.2.cloned.1.call-start = ((), (), s32[]{:S(2)}) async-start(), calls=%async_computation.2 | async-start | bytes 5242880 | tf_op jit(solution)/shard_map/all_gather | solution.py:49
  10.2 5.0 %copy-start.4 = (f32[16,64,4,128]{3,0,2,1:T(8,128)}, f32[16,64,4,128]{3,0,2,1:T(8,128)S(1)}, u32[]{:S(2)}) copy-start(f32[16,64,4,128]{3,0,2,1:T(8,128)S(1)} %copy.52) | copy-start | bytes 6291460
  10.2 3.7 %collective-permute-start.1 = (f32[16,1,4,128]{3,0,2,1:T(8,128)S(1)}, f32[16,1,4,128]{3,0,2,1:T(8,128)S(1)}, u32[]{:S(2)}, u32[]{:S(2)}) collective-permute-start(f32[16,1,4,128]{3,0,2,1:T(8,128)S(1)} %get-tuple-element.17), channel_id=1, source_target_pairs={{0,8},{8,16},{16,24},{1,9},{9,17},{17,25},{2,10},{10,18},{18,26},{... | collective-permute-start | bytes 98312 | tf_op jit(solution)/shard_map/ppermute | solution.py:14
  12.6 5.2 %collective-permute-start = (f32[16,1,4,128]{3,0,2,1:T(8,128)S(1)}, f32[16,1,4,128]{3,0,2,1:T(8,128)S(1)}, u32[]{:S(2)}, u32[]{:S(2)}) collective-permute-start(f32[16,1,4,128]{3,0,2,1:T(8,128)S(1)} %get-tuple-element.16), channel_id=1, source_target_pairs={{8,0},{16,8},{24,16},{9,1},{17,9},{25,17},{10,2},{18,10},{26,18},{... | collective-permute-start | bytes 98312 | tf_op jit(solution)/shard_map/ppermute | solution.py:17
  13.9 1.3 copy-start.11
  17.8 15.5 %copy-start.13 = (f32[16,1,4,128]{3,0,2,1:T(8,128)}, f32[16,1,4,128]{3,0,2,1:T(8,128)S(1)}, u32[]{:S(2)}) copy-start(f32[16,1,4,128]{3,0,2,1:T(8,128)S(1)} %collective-permute-done) | copy-start | bytes 98308
  17.8 17.2 %copy-start.2 = (f32[16,66,4,128]{3,0,2,1:T(8,128)}, f32[16,66,4,128]{3,0,2,1:T(8,128)S(1)}, u32[]{:S(2)}) copy-start(f32[16,66,4,128]{3,0,2,1:T(8,128)S(1)} %constant_dynamic-update-slice_fusion) | copy-start | bytes 6488068
  17.9 15.4 %collective-permute-start.2 = (f32[16,66,1,128]{3,0,2,1:T(8,128)S(1)}, f32[16,66,1,128]{3,0,2,1:T(8,128)S(1)}, u32[]{:S(2)}, u32[]{:S(2)}) collective-permute-start(f32[16,66,1,128]{3,0,2,1:T(8,128)S(1)} %get-tuple-element.15), channel_id=1, source_target_pairs={{4,0},{5,1},{6,2},{7,3},{12,8},{13,9},{14,10},{15,11},{20,16},{21,... | collective-permute-start | bytes 1622024 | tf_op jit(solution)/shard_map/ppermute | solution.py:17
  19.2 15.9 %collective-permute-start.3 = (f32[16,66,1,128]{3,0,2,1:T(8,128)S(1)}, f32[16,66,1,128]{3,0,2,1:T(8,128)S(1)}, u32[]{:S(2)}, u32[]{:S(2)}) collective-permute-start(f32[16,66,1,128]{3,0,2,1:T(8,128)S(1)} %get-tuple-element.14), channel_id=1, source_target_pairs={{0,4},{1,5},{2,6},{3,7},{8,12},{9,13},{10,14},{11,15},{16,20},{17,... | collective-permute-start | bytes 1622024 | tf_op jit(solution)/shard_map/ppermute | solution.py:14
  33.3 1.8 copy-start.6
  41.8 10.4 %collective-permute-start.4 = (f32[16,66,6,1]{1,0,3,2:T(8,128)S(1)}, f32[16,66,6,1]{1,0,3,2:T(8,128)S(1)}, u32[]{:S(2)}, u32[]{:S(2)}) collective-permute-start(f32[16,66,6,1]{1,0,3,2:T(8,128)S(1)} %copy.45), channel_id=1, source_target_pairs={{1,0},{2,1},{3,2},{5,4},{6,5},{7,6},{9,8},{10,9},{11,10},{13,12},{... | collective-permute-start | bytes 76040 | tf_op jit(solution)/shard_map/ppermute | solution.py:17
  45.3 9.6 %collective-permute-start.5 = (f32[16,66,6,1]{1,0,3,2:T(8,128)}, f32[16,66,6,1]{1,0,3,2:T(8,128)}, u32[]{:S(2)}, u32[]{:S(2)}) collective-permute-start(f32[16,66,6,1]{1,0,3,2:T(8,128)} %copy.47), channel_id=1, source_target_pairs={{0,1},{1,2},{2,3},{4,5},{5,6},{6,7},{8,9},{9,10},{10,11},{12,13},{... | collective-permute-start | bytes 76040 | tf_op jit(solution)/shard_map/ppermute | solution.py:14
  54.9 3.6 %copy-start.3 = (f32[16,66,4,128]{3,0,2,1:T(8,128)S(1)}, f32[16,66,4,128]{3,0,2,1:T(8,128)}, u32[]{:S(2)}) copy-start(f32[16,66,4,128]{3,0,2,1:T(8,128)} %copy-done.2) | copy-start | bytes 6488068
  54.9 3.6 %copy-start.7 = (f32[16,66,1,128]{3,0,2,1:T(8,128)S(1)}, f32[16,66,1,128]{3,0,2,1:T(8,128)}, u32[]{:S(2)}) copy-start(f32[16,66,1,128]{3,0,2,1:T(8,128)} %copy-done.6) | copy-start | bytes 1622020
  54.9 3.6 %copy-start.9 = (f32[16,66,1,128]{3,0,2,1:T(8,128)S(1)}, f32[16,66,1,128]{3,0,2,1:T(8,128)}, u32[]{:S(2)}) copy-start(f32[16,66,1,128]{3,0,2,1:T(8,128)} %copy-done.8) | copy-start | bytes 1622020
  54.9 3.6 %copy-start.12 = (f32[16,1,4,128]{3,0,2,1:T(8,128)S(1)}, f32[16,1,4,128]{3,0,2,1:T(8,128)}, u32[]{:S(2)}) copy-start(f32[16,1,4,128]{3,0,2,1:T(8,128)} %copy-done.11) | copy-start | bytes 98308
  54.9 3.6 %copy-start.14 = (f32[16,16]{1,0:T(8,128)S(1)}, f32[16,16]{1,0:T(8,128)}, u32[]{:S(2)}) copy-start(f32[16,16]{1,0:T(8,128)} %param.11) | copy-start | bytes 3076
  54.9 3.6 %copy-start.15 = (f32[16]{0:T(128)S(1)}, f32[16]{0:T(128)}, u32[]{:S(2)}) copy-start(f32[16]{0:T(128)} %param.10) | copy-start | bytes 196
  69.1 122.2 %reduce-scatter.2.cloned.1.call-start = ((), (), s32[]{:S(2)}) async-start(), calls=%async_computation.3 | async-start | bytes 1179648 | tf_op jit(solution)/shard_map/reduce_scatter | solution.py:53
  163.9 5.7 %copy-start.5 = (f32[16,64,4,128]{3,0,2,1:T(8,128)S(1)}, f32[16,64,4,128]{3,0,2,1:T(8,128)}, u32[]{:S(2)}) copy-start(f32[16,64,4,128]{3,0,2,1:T(8,128)} %get-tuple-element.22) | copy-start | bytes 6291460
  166.1 13.8 %all-to-all-start = ((bf16[64,4,1024]{2,0,1:T(8,128)(2,1)}), bf16[64,4,1024]{2,0,1:T(8,128)(2,1)S(1)}, u32[]{:S(2)}, u32[]{:S(2)}) async-start(bf16[64,4,1024]{2,0,1:T(8,128)(2,1)} %reshape.22), calls=%async_computation.1 | async-start | bytes 1048576 | tf_op jit(solution)/shard_map/all_to_all | solution.py:66
  169.6 10.6 %copy-start.10 = (f32[256,64]{0,1:T(8,128)S(1)}, f32[256,64]{0,1:T(8,128)}, u32[]{:S(2)}) copy-start(f32[256,64]{0,1:T(8,128)} %param.13) | copy-start | bytes 196612
  (1 other events, 0.8 us)
Sparse Core Ops, SparseCore 0:
  69.3 80.7 all-gather.1
  157.1 34.1 reduce-scatter.1
where the time goes:
time: 200 us
  waiting for transfers between devices  113 us (56%)
  matrix products  25.7 us (13%)
  local copies, waits for them, and re-layouts  25.3 us (13%)
  starting transfers between devices  19.8 us (10%)
  between operations  14.3 us (7%)
    all_gather x1, waiting for transfers between devices, shards(): gathered = lax.all_gather(snapshot, 'ga', axis=3, tiled=True)  80.7 us
    ppermute x3, starting transfers between devices, with_halo(): lax.ppermute(lax.slice_in_dim(block, block.shape[dim] - width, None, axis...  12.2 us
    ppermute x3, waiting for transfers between devices, with_halo(): lax.ppermute(lax.slice_in_dim(block, 0, width, axis=dim), axis, backward)  12.1 us
    dot_general x1, matrix products, shards(): jnp.einsum('vw,wyzx->vyzx', reaction, fields, precision=lax.Precision.HIG...  10.6 us
    reduce_scatter x1, waiting for transfers between devices, shards(): lax.psum_scatter(lax.dot_general(unfolded, unfolded, (((0,), (0,)), ((),...  10.1 us
    all_to_all x1, waiting for transfers between devices, shards(): lax.all_to_all(projected, 'gy', split_axis=1, concat_axis=0, tiled=True)  8.14 us
    unnamed x36, local copies, waits for them, and re-layouts  7.19 us
    dot_general x1, matrix products, shards(): jnp.einsum('vyzx,xr->yzvr', gathered, x_factor, preferred_element_type=jn...  6.91 us
  transfers between devices with their start and end apart: 9, of which 6 were waited for; matrix products, arithmetic and copies ran while one was open for 10% of the time, Pallas kernels for 0%

commit v1 on v0

--- a/solution.py
+++ b/solution.py
@@ -46,7 +46,9 @@
     snapshot = new_fields.astype(jnp.bfloat16)
     devices = lax.axis_size("gy") * lax.axis_size("gz")
     rank_x = x_factor.shape[1]
-    gathered = lax.all_gather(snapshot, "ga", axis=3, tiled=True)
+    gathered = jnp.concatenate(
+        lax.all_to_all(jnp.stack([snapshot] * lax.axis_size("ga")), "ga", 0, 0), axis=3
+    )
     variables, y_cells, z_cells, x_cells = gathered.shape
     unfolded = gathered.reshape(variables * y_cells * z_cells, x_cells)
     cell_count = float(variables * y_cells * z_cells * devices)

time: 200 us -> 224 us (1.12)
  blocking collectives: 0 us -> 97.3 us
  waiting for transfers between devices: 113 us -> 21.9 us
  local copies, waits for them, and re-layouts: 25.3 us -> 50.2 us
  matrix products: 25.7 us -> 18.3 us
    all_to_all x0 -> x1, blocking collectives: none -> 97.3 us  [shards(): lax.all_to_all(jnp.stack([snapshot] * lax.axis_size('ga')), 'ga', 0, 0)]
    all_gather x1 -> x0, waiting for transfers between devices: 80.7 us -> none  [shards(): gathered = lax.all_gather(snapshot, 'ga', axis=3, tiled=True)]
    reshape x0 -> x3, local copies, waits for them, and re-layouts: none -> 22.3 us  [shards(): jnp.concatenate(lax.all_to_all(jnp.stack([snapshot] * lax.axis_size('ga')...]
    reduce_scatter x1, waiting for transfers between devices: 10.1 us -> 0.01 us  [shards(): lax.psum_scatter(lax.dot_general(unfolded, unfolded, (((0,), (0,)), ((),...]
    dot_general x1, matrix products: 6.83 us -> 3.34 us  [shards(): lax.dot_general(unfolded, unfolded, (((0,), (0,)), ((), ())), preferred_e...]
    dot_general x1, matrix products: 6.91 us -> 3.42 us  [shards(): jnp.einsum('vyzx,xr->yzvr', gathered, x_factor, preferred_element_type=jn...]
    unnamed x36 -> x38, local copies, waits for them, and re-layouts: 7.19 us -> 7.2 us
  transfers between devices with their start and end apart: 9 -> 8, of which waited for: 6 -> 4; matrix products, arithmetic and copies ran while one was open for 10% -> 15% of each run, Pallas kernels for 0% -> 0%
where the time goes in v1:
time: 224 us; the launch traced here: 223 us
  blocking collectives  97.3 us (43%)
  local copies, waits for them, and re-layouts  50.2 us (22%)
  waiting for transfers between devices  21.9 us (10%)
  starting transfers between devices  19.5 us (9%)
  matrix products  18.3 us (8%)
  between operations  14.3 us (6%)
    all_to_all x1, blocking collectives, shards(): lax.all_to_all(jnp.stack([snapshot] * lax.axis_size('ga')), 'ga', 0, 0)  97.3 us
    reshape x3, local copies, waits for them, and re-layouts, shards(): jnp.concatenate(lax.all_to_all(jnp.stack([snapshot] * lax.axis_size('ga')...  22.3 us
    ppermute x3, starting transfers between devices, with_halo(): lax.ppermute(lax.slice_in_dim(block, block.shape[dim] - width, None, axis...  12.2 us
    ppermute x3, waiting for transfers between devices, with_halo(): lax.ppermute(lax.slice_in_dim(block, 0, width, axis=dim), axis, backward)  12.1 us
    dot_general x1, matrix products, shards(): jnp.einsum('vw,wyzx->vyzx', reaction, fields, precision=lax.Precision.HIG...  10.2 us
    all_to_all x1, waiting for transfers between devices, shards(): lax.all_to_all(projected, 'gy', split_axis=1, concat_axis=0, tiled=True)  8.03 us
    unnamed x38, local copies, waits for them, and re-layouts  7.2 us
    slice x3, local copies, waits for them, and re-layouts, with_halo(): lax.slice_in_dim(block, 0, width, axis=dim)  5.66 us
  transfers between devices with their start and end apart: 8, of which 4 were waited for; matrix products, arithmetic and copies ran while one was open for 15% of the time, Pallas kernels for 0%

profile of v1, /device:TPU:0, one launch (start us, length us, event | category | flops | bytes accessed | tf_op | source)
XLA Modules:
  0.0 223.4 jit_solution(16350344933387058608)
XLA Ops:
  7.2 3.0 %copy.49 = f32[16,64,4,128]{3,0,2,1:T(8,128)S(1)} copy(f32[16,64,4,128]{3,2,1,0:T(4,128)} %param.7) | data formatting | bytes 4194304 | tf_op args[0]
  10.2 2.4 %collective-permute-start.1 = (f32[16,1,4,128]{3,0,2,1:T(8,128)S(1)}, f32[16,1,4,128]{3,0,2,1:T(8,128)S(1)}, u32[]{:S(2)}, u32[]{:S(2)}) collective-permute-start(f32[16,1,4,128]{3,0,2,1:T(8,128)S(1)} %get-tuple-element.17), channel_id=1, source_target_pairs={{0,8},{8,16},{16,24},{1,9},{9,17},{17,25},{2,10},{10,18},{18,26},{... | collective-permute-start | bytes 98312 | tf_op jit(solution)/shard_map/ppermute | solution.py:14
  15.2 2.6 %collective-permute-done = f32[16,1,4,128]{3,0,2,1:T(8,128)S(1)} collective-permute-done((f32[16,1,4,128]{3,0,2,1:T(8,128)S(1)}, f32[16,1,4,128]{3,0,2,1:T(8,128)S(1)}, u32[]{:S(2)}, u32[]{:S(2)}) %collective-permute-start) | collective-permute-done | bytes 32800 | tf_op jit(solution)/shard_map/ppermute | solution.py:17
  19.2 4.6 %collective-permute-start.3 = (f32[16,66,1,128]{3,0,2,1:T(8,128)S(1)}, f32[16,66,1,128]{3,0,2,1:T(8,128)S(1)}, u32[]{:S(2)}, u32[]{:S(2)}) collective-permute-start(f32[16,66,1,128]{3,0,2,1:T(8,128)S(1)} %get-tuple-element.14), channel_id=1, source_target_pairs={{0,4},{1,5},{2,6},{3,7},{8,12},{9,13},{10,14},{11,15},{16,20},{17,... | collective-permute-start | bytes 1622024 | tf_op jit(solution)/shard_map/ppermute | solution.py:14
  23.8 9.5 %collective-permute-done.2 = f32[16,66,1,128]{3,0,2,1:T(8,128)S(1)} collective-permute-done((f32[16,66,1,128]{3,0,2,1:T(8,128)S(1)}, f32[16,66,1,128]{3,0,2,1:T(8,128)S(1)}, u32[]{:S(2)}, u32[]{:S(2)}) %collective-permute-start.2) | collective-permute-done | bytes 540704 | tf_op jit(solution)/shard_map/ppermute | solution.py:17
  33.3 1.8 collective-permute-done.3
  36.2 2.9 %fusion.8 = (f32[16,66,6,1]{3,0,2,1:T(8,128)}, f32[16,66,6,1]{3,0,2,1:T(8,128)S(1)}) fusion(f32[16,66,6,128]{3,0,2,1:T(8,128)S(1)} %pad_maximum_fusion), kind=kLoop, calls=%fused_computation.30 | loop fusion | bytes 101376 | tf_op jit(solution)/shard_map/slice | solution.py:17
  39.0 2.8 %copy.42 = f32[16,66,6,1]{1,0,3,2:T(8,128)S(1)} copy(f32[16,66,6,1]{3,0,2,1:T(8,128)} %get-tuple-element.12) | data formatting | bytes 50688 | tf_op jit(solution)/shard_map/slice | solution.py:17
  43.1 2.2 copy.44
  45.3 5.2 %collective-permute-start.5 = (f32[16,66,6,1]{1,0,3,2:T(8,128)}, f32[16,66,6,1]{1,0,3,2:T(8,128)}, u32[]{:S(2)}, u32[]{:S(2)}) collective-permute-start(f32[16,66,6,1]{1,0,3,2:T(8,128)} %copy.44), channel_id=1, source_target_pairs={{0,1},{1,2},{2,3},{4,5},{5,6},{6,7},{8,9},{9,10},{10,11},{12,13},{... | collective-permute-start | bytes 76040 | tf_op jit(solution)/shard_map/ppermute | solution.py:14
  50.5 1.7 slice_bitcast_fusion.2
  52.2 2.8 %copy.43 = f32[16,66,6,1]{3,0,2,1:T(8,128)} copy(f32[16,66,6,1]{1,0,3,2:T(8,128)S(1)} %collective-permute-done.4) | data formatting | bytes 50688 | tf_op jit(solution)/shard_map/ppermute | solution.py:17
  55.1 3.5 %copy.45 = f32[16,66,6,1]{3,0,2,1:T(8,128)} copy(f32[16,66,6,1]{1,0,3,2:T(8,128)} %collective-permute-done.5) | data formatting | bytes 50688 | tf_op jit(solution)/shard_map/ppermute | solution.py:14
  58.6 10.2 %fusion.11 = (bf16[16,64,4,128]{3,0,2,1:T(8,128)(2,1)S(1)}, f32[16,64,4,128]{3,0,2,1:T(8,128)}) fusion(f32[16,64,4,128]{3,0,2,1:T(8,128)} %copy-done.5, f32[16,16]{1,0:T(8,128)S(1)} %copy-done.15, f32[64,4,128]{2,1,0:T(4,128)} %get-tuple-element.19, f32[64,4,128]{2,1,0:T(4,128)} %get-tuple-element.20, f32[64,4,128]{2,1,0:T(4,128)S(1)} %get-tuple-element.18, ...), kind=kOutput, calls=%fused_computation.33 | convolution fusion | flops 119537664 | bytes 11094593 | tf_op jit(solution)/shard_map/vw,wyzx->vyzx/dot_general | solution.py:41
  69.3 2.0 stack.2
  71.3 97.3 %all_to_all.20 = bf16[4,16,64,4,128]{4,3,2,1,0:T(4,128)(2,1)S(1)} all-to-all(bf16[4,16,64,4,128]{4,3,2,1,0:T(4,128)(2,1)S(1)} %stack.2), channel_id=1, replica_groups=mesh['gy'=4,'gz'=2,'ga'=4] {'ga'}, dimensions={0} | all-to-all | bytes 8388608 | tf_op jit(solution)/shard_map/all_to_all | solution.py:50
  168.6 5.8 %copy.51 = bf16[16,64,4,4,128]{4,3,2,1,0:T(4,128)(2,1)S(1)} copy(bf16[16,64,4,4,128]{4,2,1,0,3:T(4,128)(2,1)S(1)} %bitcast.45) | data formatting | bytes 8388608 | tf_op jit(solution)/shard_map/reshape | solution.py:49
  174.5 3.3 %fusion = f32[512,512]{1,0:T(8,128)} fusion(bf16[512,8,4,128]{3,2,1,0:T(4,128)(2,1)S(1)} %bitcast.48), kind=kOutput, calls=%fused_computation | convolution fusion | flops 2147483648 | bytes 5242880 | tf_op jit(solution)/shard_map/dot_general | solution.py:56
  177.9 9.2 %copy.52 = bf16[16,64,4,4,128]{4,3,1,2,0:T(4,128)(2,1)} copy(bf16[16,64,4,4,128]{4,2,1,0,3:T(4,128)(2,1)} %bitcast.46) | data formatting | bytes 8388608 | tf_op jit(solution)/shard_map/reshape | solution.py:49
  187.1 7.2 %reshape.30 = bf16[16,64,4,512]{3,1,2,0:T(8,128)(2,1)} reshape(bf16[16,64,4,4,128]{4,3,1,2,0:T(4,128)(2,1)} %copy.52) | data formatting | bytes 8388608 | tf_op jit(solution)/shard_map/reshape | solution.py:49
  194.3 3.4 %fusion.5 = bf16[64,4,16,64]{3,0,1,2:T(8,128)(2,1)S(1)} fusion(bf16[16,64,4,512]{3,1,2,0:T(8,128)(2,1)} %reshape.30, bf16[512,64]{0,1:T(8,128)(2,1)S(1)} %copy-done), kind=kOutput, calls=%fused_computation.18 | convolution fusion | flops 268697600 | bytes 4784128 | tf_op jit(solution)/shard_map/vyzx,xr->yzvr/dot_general | solution.py:64
  200.0 3.5 %all-to-all-start.1 = ((bf16[64,4,1024]{2,0,1:T(8,128)(2,1)}), bf16[64,4,1024]{2,0,1:T(8,128)(2,1)S(1)}, u32[]{:S(2)}, u32[]{:S(2)}) async-start(bf16[64,4,1024]{2,0,1:T(8,128)(2,1)} %reshape.31), calls=%async_computation.2 | async-start | bytes 1048576 | tf_op jit(solution)/shard_map/all_to_all | solution.py:68
  203.5 2.1 copy.54
  205.6 8.0 %all-to-all-done.1 = bf16[64,4,1024]{2,0,1:T(8,128)(2,1)S(1)} async-done(((bf16[64,4,1024]{2,0,1:T(8,128)(2,1)}), bf16[64,4,1024]{2,0,1:T(8,128)(2,1)S(1)}, u32[]{:S(2)}, u32[]{:S(2)}) %all-to-all-start.1) | async-done | bytes 524320 | tf_op jit(solution)/shard_map/all_to_all | solution.py:68
  (55 shorter events, 12.1 us)
Async XLA Ops:
  7.2 187.1 %copy-start = (bf16[512,64]{0,1:T(8,128)(2,1)S(1)}, bf16[512,64]{0,1:T(8,128)(2,1)}, u32[]{:S(2)}) copy-start(bf16[512,64]{0,1:T(8,128)(2,1)} %param.12) | copy-start | bytes 196612
  7.2 6.8 %copy-start.2 = (f32[16,64,4,128]{3,2,1,0:T(4,128)S(1)}, f32[16,64,4,128]{3,2,1,0:T(4,128)}, u32[]{:S(2)}) copy-start(f32[16,64,4,128]{3,2,1,0:T(4,128)} %param.7) | copy-start | bytes 6291460
  7.2 207.8 %reduce-scatter.2.cloned.1.call-start = ((), (), s32[]{:S(2)}) async-start(), calls=%async_computation.3 | async-start | bytes 1179648 | tf_op jit(solution)/shard_map/reduce_scatter | solution.py:55
  10.2 5.0 %copy-start.5 = (f32[16,64,4,128]{3,0,2,1:T(8,128)}, f32[16,64,4,128]{3,0,2,1:T(8,128)S(1)}, u32[]{:S(2)}) copy-start(f32[16,64,4,128]{3,0,2,1:T(8,128)S(1)} %copy.49) | copy-start | bytes 6291460
  10.2 3.7 %collective-permute-start.1 = (f32[16,1,4,128]{3,0,2,1:T(8,128)S(1)}, f32[16,1,4,128]{3,0,2,1:T(8,128)S(1)}, u32[]{:S(2)}, u32[]{:S(2)}) collective-permute-start(f32[16,1,4,128]{3,0,2,1:T(8,128)S(1)} %get-tuple-element.17), channel_id=1, source_target_pairs={{0,8},{8,16},{16,24},{1,9},{9,17},{17,25},{2,10},{10,18},{18,26},{... | collective-permute-start | bytes 98312 | tf_op jit(solution)/shard_map/ppermute | solution.py:14
  12.6 5.2 %collective-permute-start = (f32[16,1,4,128]{3,0,2,1:T(8,128)S(1)}, f32[16,1,4,128]{3,0,2,1:T(8,128)S(1)}, u32[]{:S(2)}, u32[]{:S(2)}) collective-permute-start(f32[16,1,4,128]{3,0,2,1:T(8,128)S(1)} %get-tuple-element.16), channel_id=1, source_target_pairs={{8,0},{16,8},{24,16},{9,1},{17,9},{25,17},{10,2},{18,10},{26,18},{... | collective-permute-start | bytes 98312 | tf_op jit(solution)/shard_map/ppermute | solution.py:17
  13.9 1.3 copy-start.12
  17.8 15.5 %copy-start.14 = (f32[16,1,4,128]{3,0,2,1:T(8,128)}, f32[16,1,4,128]{3,0,2,1:T(8,128)S(1)}, u32[]{:S(2)}) copy-start(f32[16,1,4,128]{3,0,2,1:T(8,128)S(1)} %collective-permute-done) | copy-start | bytes 98308
  17.8 17.2 %copy-start.3 = (f32[16,66,4,128]{3,0,2,1:T(8,128)}, f32[16,66,4,128]{3,0,2,1:T(8,128)S(1)}, u32[]{:S(2)}) copy-start(f32[16,66,4,128]{3,0,2,1:T(8,128)S(1)} %constant_dynamic-update-slice_fusion) | copy-start | bytes 6488068
  17.9 15.4 %collective-permute-start.2 = (f32[16,66,1,128]{3,0,2,1:T(8,128)S(1)}, f32[16,66,1,128]{3,0,2,1:T(8,128)S(1)}, u32[]{:S(2)}, u32[]{:S(2)}) collective-permute-start(f32[16,66,1,128]{3,0,2,1:T(8,128)S(1)} %get-tuple-element.15), channel_id=1, source_target_pairs={{4,0},{5,1},{6,2},{7,3},{12,8},{13,9},{14,10},{15,11},{20,16},{21,... | collective-permute-start | bytes 1622024 | tf_op jit(solution)/shard_map/ppermute | solution.py:17
  19.2 15.9 %collective-permute-start.3 = (f32[16,66,1,128]{3,0,2,1:T(8,128)S(1)}, f32[16,66,1,128]{3,0,2,1:T(8,128)S(1)}, u32[]{:S(2)}, u32[]{:S(2)}) collective-permute-start(f32[16,66,1,128]{3,0,2,1:T(8,128)S(1)} %get-tuple-element.14), channel_id=1, source_target_pairs={{0,4},{1,5},{2,6},{3,7},{8,12},{9,13},{10,14},{11,15},{16,20},{17,... | collective-permute-start | bytes 1622024 | tf_op jit(solution)/shard_map/ppermute | solution.py:14
  33.3 1.8 copy-start.7
  41.8 10.4 %collective-permute-start.4 = (f32[16,66,6,1]{1,0,3,2:T(8,128)S(1)}, f32[16,66,6,1]{1,0,3,2:T(8,128)S(1)}, u32[]{:S(2)}, u32[]{:S(2)}) collective-permute-start(f32[16,66,6,1]{1,0,3,2:T(8,128)S(1)} %copy.42), channel_id=1, source_target_pairs={{1,0},{2,1},{3,2},{5,4},{6,5},{7,6},{9,8},{10,9},{11,10},{13,12},{... | collective-permute-start | bytes 76040 | tf_op jit(solution)/shard_map/ppermute | solution.py:17
  45.3 9.7 %collective-permute-start.5 = (f32[16,66,6,1]{1,0,3,2:T(8,128)}, f32[16,66,6,1]{1,0,3,2:T(8,128)}, u32[]{:S(2)}, u32[]{:S(2)}) collective-permute-start(f32[16,66,6,1]{1,0,3,2:T(8,128)} %copy.44), channel_id=1, source_target_pairs={{0,1},{1,2},{2,3},{4,5},{5,6},{6,7},{8,9},{9,10},{10,11},{12,13},{... | collective-permute-start | bytes 76040 | tf_op jit(solution)/shard_map/ppermute | solution.py:14
  55.0 3.5 %copy-start.4 = (f32[16,66,4,128]{3,0,2,1:T(8,128)S(1)}, f32[16,66,4,128]{3,0,2,1:T(8,128)}, u32[]{:S(2)}) copy-start(f32[16,66,4,128]{3,0,2,1:T(8,128)} %copy-done.3) | copy-start | bytes 6488068
  55.0 3.5 %copy-start.8 = (f32[16,66,1,128]{3,0,2,1:T(8,128)S(1)}, f32[16,66,1,128]{3,0,2,1:T(8,128)}, u32[]{:S(2)}) copy-start(f32[16,66,1,128]{3,0,2,1:T(8,128)} %copy-done.7) | copy-start | bytes 1622020
  55.0 3.5 %copy-start.10 = (f32[16,66,1,128]{3,0,2,1:T(8,128)S(1)}, f32[16,66,1,128]{3,0,2,1:T(8,128)}, u32[]{:S(2)}) copy-start(f32[16,66,1,128]{3,0,2,1:T(8,128)} %copy-done.9) | copy-start | bytes 1622020
  55.0 3.5 %copy-start.13 = (f32[16,1,4,128]{3,0,2,1:T(8,128)S(1)}, f32[16,1,4,128]{3,0,2,1:T(8,128)}, u32[]{:S(2)}) copy-start(f32[16,1,4,128]{3,0,2,1:T(8,128)} %copy-done.12) | copy-start | bytes 98308
  55.0 3.6 %copy-start.15 = (f32[16,16]{1,0:T(8,128)S(1)}, f32[16,16]{1,0:T(8,128)}, u32[]{:S(2)}) copy-start(f32[16,16]{1,0:T(8,128)} %param.11) | copy-start | bytes 3076
  55.0 3.5 %copy-start.16 = (f32[16]{0:T(128)S(1)}, f32[16]{0:T(128)}, u32[]{:S(2)}) copy-start(f32[16]{0:T(128)} %param.10) | copy-start | bytes 196
  168.6 5.8 %copy-start.1 = (bf16[4,16,64,4,128]{4,3,2,1,0:T(4,128)(2,1)}, bf16[4,16,64,4,128]{4,3,2,1,0:T(4,128)(2,1)S(1)}, u32[]{:S(2)}) copy-start(bf16[4,16,64,4,128]{4,3,2,1,0:T(4,128)(2,1)S(1)} %all_to_all.20) | copy-start | bytes 12582916
  197.7 5.7 %copy-start.6 = (f32[16,64,4,128]{3,0,2,1:T(8,128)S(1)}, f32[16,64,4,128]{3,0,2,1:T(8,128)}, u32[]{:S(2)}) copy-start(f32[16,64,4,128]{3,0,2,1:T(8,128)} %get-tuple-element.22) | copy-start | bytes 6291460
  200.0 13.7 %all-to-all-start.1 = ((bf16[64,4,1024]{2,0,1:T(8,128)(2,1)}), bf16[64,4,1024]{2,0,1:T(8,128)(2,1)S(1)}, u32[]{:S(2)}, u32[]{:S(2)}) async-start(bf16[64,4,1024]{2,0,1:T(8,128)(2,1)} %reshape.31), calls=%async_computation.2 | async-start | bytes 1048576 | tf_op jit(solution)/shard_map/all_to_all | solution.py:68
  203.5 10.5 %copy-start.11 = (f32[256,64]{0,1:T(8,128)S(1)}, f32[256,64]{0,1:T(8,128)}, u32[]{:S(2)}) copy-start(f32[256,64]{0,1:T(8,128)} %param.13) | copy-start | bytes 196612
  (1 other events, 0.8 us)
Sparse Core Ops, SparseCore 0:
  178.0 36.0 reduce-scatter.1
